TPU v7x, 32 devices: a whole 2x2x4 slice. The times are simulated.
32 devices in a mesh: wide: 8 (over z, x), narrow: 4 (over y, core).
Axes of the slice: x: 2, y: 2, z: 4, core: 2. Of those that a mesh axis runs over, the one named last changes fastest.
Arguments:
- block_input: bfloat16 [12288, 768], P('wide')
- cotangent: bfloat16 [12288, 768], P('wide'), may hold values from -6 to 6
- lengths: int32 [16, 12], P('wide'), may hold values from 0 to 384, as said below
- project_weight: float32 [3, 768, 768], P(None, 'wide', 'narrow'), may hold values from -0.125 to 0.125
- output_weight: float32 [768, 768], P('narrow', 'wide'), may hold values from -1.25 to 1.25
- expand_weight: float32 [2, 768, 2048], P(None, 'wide', 'narrow'), may hold values from -0.21875 to 0.21875
- shrink_weight: float32 [2048, 768], P('narrow', 'wide'), may hold values from -0.1875 to 0.1875
- bucket_bias: float32 [32, 12], replicated, may hold values from -3 to 3
- norm_gains: float32 [2, 768], P(None, 'wide'), may hold values from 0.5 to 1.5
- project_first: float32 [3, 768, 768], P(None, 'wide', 'narrow'), may hold values from -0.00061035156 to 0.00061035156
- output_first: float32 [768, 768], P('narrow', 'wide'), may hold values from -7.6293945e-05 to 7.6293945e-05
- expand_first: float32 [2, 768, 2048], P(None, 'wide', 'narrow'), may hold values from -0.00015258789 to 0.00015258789
- shrink_first: float32 [2048, 768], P('narrow', 'wide'), may hold values from -0.00015258789 to 0.00015258789
- bucket_first: float32 [32, 12], replicated, may hold values from -0.00010681152 to 0.00010681152
- gains_first: float32 [2, 768], P(None, 'wide'), may hold values from -0.00048828125 to 0.00048828125
- project_second: float32 [3, 768, 768], P(None, 'wide', 'narrow'), may hold values from 4.3798376e-10 to 7.064254e-09
- output_second: float32 [768, 768], P('narrow', 'wide'), may hold values from 6.3578288e-12 to 1.0172526e-10
- expand_second: float32 [2, 768, 2048], P(None, 'wide', 'narrow'), may hold values from 2.5431315e-11 to 4.0972675e-10
- shrink_second: float32 [2048, 768], P('narrow', 'wide'), may hold values from 2.5431315e-11 to 4.0972675e-10
- bucket_second: float32 [32, 12], replicated, may hold values from 1.1302807e-11 to 1.8084491e-10
- gains_second: float32 [2, 768], P(None, 'wide'), may hold values from 2.8257016e-10 to 4.5211226e-09
Outputs:
- block_output: bfloat16 [12288, 768], P('wide')
- input_gradient: bfloat16 [12288, 768], P('wide')
- global_norm: float32 [], replicated
- new_project: float32 [3, 768, 768], P(None, 'wide', 'narrow')
- new_output: float32 [768, 768], P('narrow', 'wide')
- new_expand: float32 [2, 768, 2048], P(None, 'wide', 'narrow')
- new_shrink: float32 [2048, 768], P('narrow', 'wide')
- new_bucket: float32 [32, 12], replicated
- new_gains: float32 [2, 768], P(None, 'wide')
- project_first_new: float32 [3, 768, 768], P(None, 'wide', 'narrow')
- output_first_new: float32 [768, 768], P('narrow', 'wide')
- expand_first_new: float32 [2, 768, 2048], P(None, 'wide', 'narrow')
- shrink_first_new: float32 [2048, 768], P('narrow', 'wide')
- bucket_first_new: float32 [32, 12], replicated
- gains_first_new: float32 [2, 768], P(None, 'wide')
- project_second_new: float32 [3, 768, 768], P(None, 'wide', 'narrow')
- output_second_new: float32 [768, 768], P('narrow', 'wide')
- expand_second_new: float32 [2, 768, 2048], P(None, 'wide', 'narrow')
- shrink_second_new: float32 [2048, 768], P('narrow', 'wide')
- bucket_second_new: float32 [32, 12], replicated
- gains_second_new: float32 [2, 768], P(None, 'wide')
Inputs may be any that keep to these rules, and one draw needn't show every extreme that they name: Each row lists one buffer's passage lengths in packing order, each from 64 to 384, followed by zeros; a row sums to at most 768, and every row holds one passage of exactly 384 tokens.
All inputs are finite; a program needn't handle non-finite values.
Results may differ from a plain program's by a relative error of at most 0.013.
The roundings to bfloat16 on the way count: a program that leaves them out, or rounds other values in their place, can miss the bound.
Values may be sent and summed in bfloat16 or wider, within the bound.
A program may use at most 128 MiB of HBM per device.

v0:
```python
import jax
import jax.numpy as jnp
from jax import lax
from jax.sharding import PartitionSpec as P

DH = 64
STEP = 10
bucket_edges = (12, 16, 23, 32, 46, 64, 91)
norm_eps = 1e-06
clip_limit = 1.0
beta_one = 0.9
beta_two = 0.999
adam_eps = 1e-08
step_rates = (0.06, 0.3, 0.07, 0.06, 1.0, 0.3)
decay_rates = (0.01, 0.01, 0.01, 0.01, 0.0, 0.0)
masked_score = -1000000000.0


def bucket_of(offsets):
    distance = jnp.abs(offsets)
    far_bucket = 8 + sum(((distance >= threshold).astype(jnp.int32) for threshold in bucket_edges))
    return jnp.where(distance < 8, distance, far_bucket) + 16 * (offsets > 0).astype(jnp.int32)


def rms_scale(values):
    return lax.rsqrt(jnp.mean(values * values, axis=-1, keepdims=True) + norm_eps)


def norm_back(values, scale_vec, gain_vec, upstream):
    weighted = upstream * gain_vec
    inner_mean = jnp.mean(weighted * values, axis=-1, keepdims=True)
    return scale_vec * weighted - values * (scale_vec * scale_vec * scale_vec) * inner_mean


def toeplitz_rows(values, length):
    padded = jnp.concatenate([values, jnp.zeros((1,), values.dtype)])
    tiled_flat = jnp.tile(padded, length)[: length * (2 * length - 1)]
    return tiled_flat.reshape(length, 2 * length - 1)[:, length - 1 :]


def diagonal_sums(matrix, length):
    padded = jnp.pad(matrix, ((0, 0), (length - 1, 1)))
    flat_vals = jnp.concatenate([padded.reshape(-1), jnp.zeros((length,), matrix.dtype)])
    return jnp.sum(flat_vals.reshape(length, 2 * length + 1), axis=0)[: 2 * length - 1]


def adam_update(weight, moment_one, moment_two, gradient, step_rate, decay_rate):
    new_first = beta_one * moment_one + (1.0 - beta_one) * gradient
    new_second = beta_two * moment_two + (1.0 - beta_two) * gradient * gradient
    first_hat = new_first / (1.0 - beta_one**STEP)
    second_hat = new_second / (1.0 - beta_two**STEP)
    new_weight = weight - step_rate * (
        first_hat / (jnp.sqrt(second_hat) + adam_eps) + decay_rate * weight
    )
    return (new_weight, new_first, new_second)


def body(
    block_input,
    cotangent,
    lengths,
    project_weight,
    output_weight,
    expand_weight,
    shrink_weight,
    bucket_bias,
    norm_gains,
    project_first,
    output_first,
    expand_first,
    shrink_first,
    bucket_first,
    gains_first,
    project_second,
    output_second,
    expand_second,
    shrink_second,
    bucket_second,
    gains_second,
):
    tokens, model_width = block_input.shape
    buffers = lengths.shape[0]
    length = tokens // buffers
    head_width = project_weight.shape[2]
    heads_local = head_width // DH
    hidden_local = expand_weight.shape[2]
    low_gains = norm_gains.astype(jnp.bfloat16)
    project_all, output_all, expand_all, shrink_all, gains_all = (
        lax.all_gather(project_weight.astype(jnp.bfloat16), "wide", axis=1, tiled=True),
        lax.all_gather(output_weight.astype(jnp.bfloat16), "wide", axis=1, tiled=True),
        lax.all_gather(expand_weight.astype(jnp.bfloat16), "wide", axis=1, tiled=True),
        lax.all_gather(shrink_weight.astype(jnp.bfloat16), "wide", axis=1, tiled=True),
        lax.all_gather(low_gains, "wide", axis=1, tiled=True),
    )
    gain_one = gains_all[0].astype(jnp.float32)
    gain_two = gains_all[1].astype(jnp.float32)
    positions = jnp.arange(length, dtype=jnp.int32)
    segment_ends = jnp.cumsum(lengths, axis=1)
    segment_ids = jnp.sum(
        (positions[None, :, None] >= segment_ends[:, None, :]).astype(jnp.int32), axis=2
    )
    offsets = jnp.arange(2 * length - 1, dtype=jnp.int32) - (length - 1)
    onehot = (
        bucket_of(offsets)[:, None] == jnp.arange(bucket_bias.shape[0], dtype=jnp.int32)[None, :]
    ).astype(jnp.float32)
    head_start = lax.axis_index("narrow") * heads_local
    bias_local = lax.dynamic_slice_in_dim(bucket_bias, head_start, heads_local, 1)
    head_bias = jnp.dot(onehot, bias_local, precision=lax.Precision.HIGHEST).T
    input_float = block_input.astype(jnp.float32)
    scale_one = rms_scale(input_float)
    normed_one = (input_float * scale_one * gain_one).astype(jnp.bfloat16)
    project_flat = jnp.transpose(project_all, (1, 0, 2)).reshape(model_width, 3 * head_width)
    qkv_rows = jnp.dot(normed_one, project_flat, preferred_element_type=jnp.float32).astype(
        jnp.bfloat16
    )
    buffer_rows = qkv_rows.reshape(buffers, length, 3 * head_width)

    def head_scores(query_rows, key_rows, bias_row, same_segment):
        scores = jnp.einsum("qd,kd->qk", query_rows, key_rows, preferred_element_type=jnp.float32)
        scores = scores + toeplitz_rows(bias_row, length)
        return jnp.where(same_segment, scores, masked_score)

    def split_heads(block_rows):
        return block_rows.reshape(length, 3, heads_local, DH).transpose(1, 2, 0, 3)

    def buffer_forward(block_items):
        block_rows, segment_row = block_items
        pieces = split_heads(block_rows)
        same_segment = segment_row[:, None] == segment_row[None, :]

        def head_forward(head_items):
            query_rows, key_rows, value_rows, bias_row = head_items
            scores = head_scores(query_rows, key_rows, bias_row, same_segment)
            row_max = jnp.max(scores, axis=1, keepdims=True)
            log_total = row_max + jnp.log(jnp.sum(jnp.exp(scores - row_max), axis=1, keepdims=True))
            attention_probs = jnp.exp(scores - log_total).astype(jnp.bfloat16)
            head_out = jnp.dot(
                attention_probs, value_rows, preferred_element_type=jnp.float32
            ).astype(jnp.bfloat16)
            return (head_out, log_total[:, 0])

        head_outs, log_rows = lax.map(head_forward, (pieces[0], pieces[1], pieces[2], head_bias))
        return (head_outs.transpose(1, 0, 2).reshape(length, head_width), log_rows)

    attended, log_totals = lax.map(buffer_forward, (buffer_rows, segment_ids))
    attended = attended.reshape(tokens, head_width)
    attention_terms = jnp.dot(attended, output_all, preferred_element_type=jnp.float32)
    middle = input_float + lax.psum(attention_terms, "narrow")
    scale_two = rms_scale(middle)
    normed_two = (middle * scale_two * gain_two).astype(jnp.bfloat16)
    expand_flat = jnp.transpose(expand_all, (1, 0, 2)).reshape(model_width, 2 * hidden_local)
    gate_up = jnp.dot(normed_two, expand_flat, preferred_element_type=jnp.float32)
    gate_pre = gate_up[:, :hidden_local]
    up_pre = gate_up[:, hidden_local:]
    activated, gelu_pull = jax.vjp(
        lambda gate_vals: jax.nn.gelu(gate_vals, approximate=True), gate_pre
    )
    hidden = (activated * up_pre).astype(jnp.bfloat16)
    feedforward_terms = jnp.dot(hidden, shrink_all, preferred_element_type=jnp.float32)
    block_output = (
        middle + lax.psum(feedforward_terms.astype(jnp.bfloat16), "narrow").astype(jnp.float32)
    ).astype(jnp.bfloat16)
    cotangent_float = cotangent.astype(jnp.float32)
    shrink_grad = jnp.einsum("tf,td->fd", hidden, cotangent, preferred_element_type=jnp.float32)
    d_hidden = jnp.einsum("td,fd->tf", cotangent, shrink_all, preferred_element_type=jnp.float32)
    d_gate = gelu_pull(d_hidden * up_pre)[0]
    d_up = d_hidden * activated
    d_gate_up = jnp.concatenate([d_gate, d_up], axis=1).astype(jnp.bfloat16)
    expand_grad = jnp.einsum("td,tf->df", normed_two, d_gate_up, preferred_element_type=jnp.float32)
    expand_grad = expand_grad.reshape(model_width, 2, hidden_local).transpose(1, 0, 2)
    second_terms = jnp.einsum(
        "tf,df->td", d_gate_up, expand_flat, preferred_element_type=jnp.float32
    )
    d_normed_two = lax.psum(second_terms, "narrow")
    gain_two_grad = jnp.sum(d_normed_two * middle * scale_two, axis=0)
    d_middle = cotangent_float + norm_back(middle, scale_two, gain_two, d_normed_two)
    d_middle_low = d_middle.astype(jnp.bfloat16)
    output_grad = jnp.einsum(
        "th,td->hd", attended, d_middle_low, preferred_element_type=jnp.float32
    )
    d_attended = jnp.einsum(
        "td,hd->th", d_middle_low, output_all, preferred_element_type=jnp.float32
    ).astype(jnp.bfloat16)

    def buffer_backward(block_items):
        block_rows, segment_row, log_row, grad_rows = block_items
        pieces = split_heads(block_rows)
        same_segment = segment_row[:, None] == segment_row[None, :]
        grad_heads = grad_rows.reshape(length, heads_local, DH).transpose(1, 0, 2)

        def head_backward(head_items):
            query_rows, key_rows, value_rows, bias_row, log_head, grad_head = head_items
            scores = head_scores(query_rows, key_rows, bias_row, same_segment)
            attention_probs = jnp.exp(scores - log_head[:, None])
            grad_probs = jnp.einsum(
                "qd,kd->qk", grad_head, value_rows, preferred_element_type=jnp.float32
            )
            grad_scores = (
                attention_probs
                * (grad_probs - jnp.sum(attention_probs * grad_probs, axis=1, keepdims=True))
            ).astype(jnp.bfloat16)
            grad_query = jnp.dot(grad_scores, key_rows, preferred_element_type=jnp.float32)
            grad_key = jnp.einsum(
                "qk,qd->kd", grad_scores, query_rows, preferred_element_type=jnp.float32
            )
            grad_value = jnp.einsum(
                "qk,qd->kd",
                attention_probs.astype(jnp.bfloat16),
                grad_head,
                preferred_element_type=jnp.float32,
            )
            grad_bias = diagonal_sums(grad_scores.astype(jnp.float32), length)
            return (jnp.stack([grad_query, grad_key, grad_value]).astype(jnp.bfloat16), grad_bias)

        grad_pieces, grad_biases = lax.map(
            head_backward, (pieces[0], pieces[1], pieces[2], head_bias, log_row, grad_heads)
        )
        return (grad_pieces.transpose(2, 1, 0, 3).reshape(length, 3 * head_width), grad_biases)

    grad_qkv, bias_rows = lax.map(
        buffer_backward,
        (buffer_rows, segment_ids, log_totals, d_attended.reshape(buffers, length, head_width)),
    )
    grad_qkv = grad_qkv.reshape(tokens, 3 * head_width)
    project_grad = jnp.einsum("td,tc->dc", normed_one, grad_qkv, preferred_element_type=jnp.float32)
    project_grad = project_grad.reshape(model_width, 3, head_width).transpose(1, 0, 2)
    first_terms = jnp.einsum(
        "tc,dc->td", grad_qkv, project_flat, preferred_element_type=jnp.float32
    )
    d_normed_one = lax.psum(first_terms, "narrow")
    gain_one_grad = jnp.sum(d_normed_one * input_float * scale_one, axis=0)
    input_gradient = (d_middle + norm_back(input_float, scale_one, gain_one, d_normed_one)).astype(
        jnp.bfloat16
    )
    local_bucket = jnp.einsum(
        "hr,rb->bh", jnp.sum(bias_rows, axis=0), onehot, precision=lax.Precision.HIGHEST
    )
    bucket_full = lax.dynamic_update_slice(
        jnp.zeros(bucket_bias.shape, jnp.float32), local_bucket, (jnp.int32(0), head_start)
    )
    project_red, output_red, expand_red, shrink_red, gains_red = (
        lax.psum_scatter(project_grad, "wide", scatter_dimension=1, tiled=True),
        lax.psum_scatter(output_grad, "wide", scatter_dimension=1, tiled=True),
        lax.psum_scatter(expand_grad, "wide", scatter_dimension=1, tiled=True),
        lax.psum_scatter(shrink_grad, "wide", scatter_dimension=1, tiled=True),
        lax.psum_scatter(
            jnp.stack([gain_one_grad, gain_two_grad]), "wide", scatter_dimension=1, tiled=True
        ),
    )
    square_sum = sum(
        (
            jnp.sum(part_grad * part_grad)
            for part_grad in (project_red, output_red, expand_red, shrink_red)
        )
    )
    square_sum = square_sum + jnp.where(
        lax.axis_index("narrow") == 0, jnp.sum(gains_red * gains_red), 0.0
    )
    square_total, bucket_grad = lax.psum((square_sum, bucket_full), ("wide", "narrow"))
    global_norm = jnp.sqrt(square_total + jnp.sum(bucket_grad * bucket_grad))
    factor = jnp.minimum(1.0, clip_limit / (global_norm + 1e-06))
    params = (project_weight, output_weight, expand_weight, shrink_weight, bucket_bias, norm_gains)
    firsts = (project_first, output_first, expand_first, shrink_first, bucket_first, gains_first)
    seconds = (
        project_second,
        output_second,
        expand_second,
        shrink_second,
        bucket_second,
        gains_second,
    )
    reduced = (project_red, output_red, expand_red, shrink_red, bucket_grad, gains_red)
    results = [
        adam_update(weight, moment_one, moment_two, factor * gradient, step_rate, decay_rate)
        for weight, moment_one, moment_two, gradient, step_rate, decay_rate in zip(
            params, firsts, seconds, reduced, step_rates, decay_rates
        )
    ]
    return (
        block_output,
        input_gradient,
        global_norm,
        results[0][0],
        results[1][0],
        results[2][0],
        results[3][0],
        results[4][0],
        results[5][0],
        results[0][1],
        results[1][1],
        results[2][1],
        results[3][1],
        results[4][1],
        results[5][1],
        results[0][2],
        results[1][2],
        results[2][2],
        results[3][2],
        results[4][2],
        results[5][2],
    )


def solution(mesh):
    in_specs = (
        P("wide", None),
        P("wide", None),
        P("wide", None),
        P(None, "wide", "narrow"),
        P("narrow", "wide"),
        P(None, "wide", "narrow"),
        P("narrow", "wide"),
        P(),
        P(None, "wide"),
        P(None, "wide", "narrow"),
        P("narrow", "wide"),
        P(None, "wide", "narrow"),
        P("narrow", "wide"),
        P(),
        P(None, "wide"),
        P(None, "wide", "narrow"),
        P("narrow", "wide"),
        P(None, "wide", "narrow"),
        P("narrow", "wide"),
        P(),
        P(None, "wide"),
    )
    out_specs = (
        P("wide", None),
        P("wide", None),
        P(),
        P(None, "wide", "narrow"),
        P("narrow", "wide"),
        P(None, "wide", "narrow"),
        P("narrow", "wide"),
        P(),
        P(None, "wide"),
        P(None, "wide", "narrow"),
        P("narrow", "wide"),
        P(None, "wide", "narrow"),
        P("narrow", "wide"),
        P(),
        P(None, "wide"),
        P(None, "wide", "narrow"),
        P("narrow", "wide"),
        P(None, "wide", "narrow"),
        P("narrow", "wide"),
        P(),
        P(None, "wide"),
    )
    return jax.shard_map(body, mesh=mesh, in_specs=in_specs, out_specs=out_specs, check_vma=False)
```

profile of v0, /device:TPU:0, one launch (start us, length us, event | category | flops | bytes accessed | tf_op | source)
XLA Modules:
  0.0 1326.2 jit_solution(2225824823571973719)
XLA Ops:
  9.7 22.1 %all-gather = bf16[8,96,2]{1,2,0:T(2,128)(2,1)S(1)} all-gather(bf16[1,96,2]{1,2,0:T(2,128)(2,1)S(1)} %convert_bitcast_fusion), channel_id=1, replica_groups=mesh['wide'=8,'narrow'=4] {'wide'}, dimensions={0}, use_global_device_ids=true | all-gather | bytes 3456 | tf_op jit(solution)/shard_map/all_gather | solution.py:93
  38.3 33.1 %all_gather.17 = bf16[192,768]{0,1:T(8,128)(2,1)} all-gather(bf16[192,96]{0,1:T(8,128)(2,1)S(1)} %copy.186), channel_id=1, replica_groups=mesh['wide'=8,'narrow'=4] {'wide'}, dimensions={1}, use_global_device_ids=true | all-gather | bytes 331776 | tf_op jit(solution)/shard_map/all_gather | solution.py:90
  71.5 35.7 %all_gather.16 = bf16[3,768,192]{2,0,1:T(4,128)(2,1)} all-gather(bf16[3,96,192]{2,0,1:T(4,128)(2,1)S(1)} %copy.181), channel_id=1, replica_groups=mesh['wide'=8,'narrow'=4] {'wide'}, dimensions={1}, use_global_device_ids=true | all-gather | bytes 995328 | tf_op jit(solution)/shard_map/all_gather | solution.py:89
  114.7 152.8 %while.65 = (s32[]{:T(128)}, bf16[2,768,192]{1,2,0:T(8,128)(2,1)}, f32[2,3,768]{2,1,0:T(4,128)}, bf16[2,768,576]{1,2,0:T(8,128)(2,1)}, s32[2,768]{1,0:T(2,128)},...) while((s32[]{:T(128)}, bf16[2,768,192]{1,2,0:T(8,128)(2,1)}, ...), condition=%wide.region_8.9_spmd, body=%wide.region_3.8_spmd.sunk | while | flops 155763456 | bytes 47086936 | solution.py:145
  116.7 73.0 %while.68 = (s32[]{:T(128)}, bf16[3,768,64]{1,2,0:T(8,128)(2,1)S(1)}, f32[3,768]{1,0:T(4,128)S(1)}, bf16[3,768,64]{1,2,0:T(8,128)(2,1)S(1)}, bf16[3,768,64]{1,2,...) while((s32[]{:T(128)}, ...), condition=%wide.region_7.7_spmd.clone, body=%wide.region_4.6_spmd.clone.sunk | while | flops 155763456 | bytes 42930292 | solution.py:142
  125.9 7.7 reshape.316
  150.3 7.7 reshape.316
  174.6 7.7 reshape.316
  193.1 73.0 %while.68 = (s32[]{:T(128)}, bf16[3,768,64]{1,2,0:T(8,128)(2,1)S(1)}, f32[3,768]{1,0:T(4,128)S(1)}, bf16[3,768,64]{1,2,0:T(8,128)(2,1)S(1)}, bf16[3,768,64]{1,2,...) while((s32[]{:T(128)}, ...), condition=%wide.region_7.7_spmd.clone, body=%wide.region_4.6_spmd.clone.sunk | while | flops 155763456 | bytes 42930292 | solution.py:142
  202.3 7.7 reshape.316
  226.7 7.7 reshape.316
  251.0 7.7 reshape.316
  275.6 33.7 %all_gather.19 = bf16[512,768]{0,1:T(8,128)(2,1)S(1)} all-gather(bf16[512,96]{0,1:T(8,128)(2,1)S(1)} %convert_element_type.180), channel_id=1, replica_groups=mesh['wide'=8,'narrow'=4] {'wide'}, dimensions={1}, use_global_device_ids=true | all-gather | bytes 884736 | tf_op jit(solution)/shard_map/all_gather | solution.py:92
  309.3 57.1 %all-reduce.8.cloned.1.call-done = f32[1536,768]{1,0:T(8,128)} async-done(((f32[1536,768]{1,0:T(8,128)}), f32[1536,768]{1,0:T(8,128)}) %all-reduce.8.cloned.1.call-update) | async-done | bytes 4718608 | tf_op jit(solution)/shard_map/psum | solution.py:148
  397.1 89.9 %all-reduce.12.cloned.1.call-done = f32[1536,768]{1,0:T(8,128)} async-done(((f32[1536,768]{1,0:T(8,128)}), f32[1536,768]{1,0:T(8,128)}) %all-reduce.12.cloned.1.call-update) | async-done | bytes 4718608 | tf_op jit(solution)/shard_map/psum | solution.py:174
  492.1 53.7 %all-reduce.10.cloned.1.call-done = bf16[1536,768]{1,0:T(8,128)(2,1)} async-done(((bf16[1536,768]{1,0:T(8,128)(2,1)}), bf16[1536,768]{1,0:T(8,128)(2,1)}) %all-reduce.10.cloned.1.call-update) | async-done | bytes 2359312 | tf_op jit(solution)/shard_map/psum | solution.py:161
  554.5 346.3 %while.67 = (s32[]{:T(128)}, bf16[2,768,576]{1,2,0:T(8,128)(2,1)}, f32[2,3,1535]{2,1,0:T(4,128)}, bf16[2,768,576]{1,2,0:T(8,128)(2,1)}, f32[2,3,768]{2,1,0:T(4,1...) while((s32[]{:T(128)}, bf16[2,768,576]{1,2,0:T(8,128)(2,1)}, ...), condition=%wide.region_19.20_spmd, body=%wide.region_14.19_spmd.sunk | while | flops 386777856 | bytes 102011568 | solution.py:220
  559.0 165.0 %while.69 = (s32[]{:T(128)}, bf16[3,3,768,64]{2,3,0,1:T(8,128)(2,1)}, f32[3,1535]{1,0:T(4,128)}, bf16[3,768,64]{1,2,0:T(8,128)(2,1)S(1)}, bf16[3,768,64]{1,2,0:T...) while((s32[]{:T(128)}, ...), condition=%wide.region_18.18_spmd.clone, body=%wide.region_15.17_spmd.clone.sunk | while | flops 386777856 | bytes 96039304 | solution.py:215
  569.6 7.7 reshape.313
  601.6 8.2 reshape.315
  656.6 8.2 reshape.315
  711.6 8.2 reshape.315
  731.9 165.0 %while.69 = (s32[]{:T(128)}, bf16[3,3,768,64]{2,3,0,1:T(8,128)(2,1)}, f32[3,1535]{1,0:T(4,128)}, bf16[3,768,64]{1,2,0:T(8,128)(2,1)S(1)}, bf16[3,768,64]{1,2,0:T...) while((s32[]{:T(128)}, ...), condition=%wide.region_18.18_spmd.clone, body=%wide.region_15.17_spmd.clone.sunk | while | flops 386777856 | bytes 96039304 | solution.py:215
  774.4 8.2 reshape.315
  829.4 8.2 reshape.315
  884.4 8.2 reshape.315
  918.4 83.8 %all-reduce.14.cloned.1.call-done = f32[1536,768]{1,0:T(8,128)} async-done(((f32[1536,768]{1,0:T(8,128)}), f32[1536,768]{1,0:T(8,128)}) %all-reduce.14.cloned.1.call-update) | async-done | bytes 4718608 | tf_op jit(solution)/shard_map/psum | solution.py:230
  1035.1 8.6 reduce-scatter.18.cloned.1.call-done
  1045.3 62.9 %reduce-scatter.20.cloned.1.call-done = f32[96,2]{1,0:T(8,128)} async-done(((f32[768,2]{1,0:T(8,128)}), f32[96,2]{1,0:T(8,128)}) %reduce-scatter.20.cloned.1.call-update) | async-done | bytes 784
  1110.3 68.5 %reduce-scatter.16.cloned.1.call-done = f32[96,576]{1,0:T(8,128)} async-done(((f32[768,576]{1,0:T(8,128)}), f32[96,576]{1,0:T(8,128)}) %reduce-scatter.16.cloned.1.call-update) | async-done | bytes 221200
  1182.1 73.7 %reduce-scatter.12.cloned.1.call-done = f32[2,96,512]{2,1,0:T(8,128)} async-done(((f32[2,768,512]{2,1,0:T(8,128)}), f32[2,96,512]{2,1,0:T(8,128)}) %reduce-scatter.12.cloned.1.call-update) | async-done | bytes 393232 | tf_op jit(solution)/shard_map/reduce_scatter | solution.py:244
  1264.5 39.9 %all-reduce.2 = (f32[]{:T(128)}, f32[32,12]{0,1:T(8,128)S(1)}) all-reduce(f32[]{:T(128)S(6)} %add.321, f32[32,12]{0,1:T(8,128)S(1)} %dynamic_update_slice.47), channel_id=1, replica_groups=mesh['wide'=8,'narrow'=4] {'wide','narrow'}, use_global_device_ids=true, to_apply=%region_34.35 | all-reduce | flops 385 | bytes 3080 | tf_op jit(solution)/shard_map/psum | solution.py:259
  (518 shorter events, 536.7 us)
Async XLA Ops:
  8.0 358.3 %all-reduce.8.cloned.1.call-start = ((), (), s32[]{:S(2)}) async-start(), calls=%async_computation.5 | async-start | bytes 9437184 | tf_op jit(solution)/shard_map/psum | solution.py:148
  8.1 104.7 %copy-start.46 = (s32[1535]{0:T(1024)}, s32[1535]{0:T(1024)S(1)}, u32[]{:S(2)}) copy-start(s32[1535]{0:T(1024)S(1)} %fusion.86) | copy-start | bytes 18424
  32.5 77.3 %copy-start.39 = (f32[768]{0:T(1024)}, f32[768]{0:T(1024)S(1)}, u32[]{:S(2)}) copy-start(f32[768]{0:T(1024)S(1)} %get-tuple-element.696) | copy-start | bytes 9220
  35.5 74.3 %copy-start.9 = (bf16[1536,768]{1,0:T(8,128)(2,1)S(1)}, bf16[1536,768]{1,0:T(8,128)(2,1)}, u32[]{:S(2)}) copy-start(bf16[1536,768]{1,0:T(8,128)(2,1)} %param.29) | copy-start | bytes 7077892
  36.1 75.3 %copy-start.34 = (f32[1536]{0:T(1024)}, f32[1536]{0:T(1024)S(1)}, u32[]{:S(2)}) copy-start(f32[1536]{0:T(1024)S(1)} %get-tuple-element.799) | copy-start | bytes 18436
  273.5 92.8 %copy-start.10 = (bf16[1536,768]{1,0:T(8,128)(2,1)S(1)}, bf16[1536,768]{1,0:T(8,128)(2,1)}, u32[]{:S(2)}) copy-start(bf16[1536,768]{1,0:T(8,128)(2,1)} %param.29) | copy-start | bytes 7077892
  273.5 98.0 %all-gather.3.cloned.1.call-start = ((), (), s32[]{:S(2)}) async-start(), calls=%async_computation.6 | async-start | bytes 1769472 | tf_op jit(solution)/shard_map/all_gather | solution.py:91
  275.5 211.6 %all-reduce.12.cloned.1.call-start = ((), (), s32[]{:S(2)}) async-start(), calls=%async_computation.8 | async-start | bytes 9437184 | tf_op jit(solution)/shard_map/psum | solution.py:174
  371.5 174.3 %copy-start.36 = (f32[1536]{0:T(1024)}, f32[1536]{0:T(1024)S(1)}, u32[]{:S(2)}) copy-start(f32[1536]{0:T(1024)S(1)} %get-tuple-element.801) | copy-start | bytes 18436
  392.7 153.1 %all-reduce.10.cloned.1.call-start = ((), (), s32[]{:S(2)}) async-start(), calls=%async_computation.7 | async-start | bytes 4718592 | tf_op jit(solution)/shard_map/psum | solution.py:161
  397.1 605.2 %all-reduce.14.cloned.1.call-start = ((), (), s32[]{:S(2)}) async-start(), calls=%async_computation.9 | async-start | bytes 9437184 | tf_op jit(solution)/shard_map/psum | solution.py:230
  559.1 25.2 %copy-start = (bf16[3,768,64]{1,2,0:T(8,128)(2,1)}, bf16[3,768,64]{1,2,0:T(8,128)(2,1)S(1)}, u32[]{:S(2)}) copy-start(bf16[3,768,64]{1,2,0:T(8,128)(2,1)S(1)} %get-tuple-element.1098) | copy-start | bytes 884740 | tf_op jit(solution)/shard_map/while/body/eval_jaxpr/while
  614.1 25.2 %copy-start = (bf16[3,768,64]{1,2,0:T(8,128)(2,1)}, bf16[3,768,64]{1,2,0:T(8,128)(2,1)S(1)}, u32[]{:S(2)}) copy-start(bf16[3,768,64]{1,2,0:T(8,128)(2,1)S(1)} %get-tuple-element.1098) | copy-start | bytes 884740 | tf_op jit(solution)/shard_map/while/body/eval_jaxpr/while
  908.0 125.5 %reduce-scatter.14.cloned.1.call-start = ((), (), s32[]{:S(2)}) async-start(), calls=%async_computation.11 | async-start | bytes 1769472 | tf_op jit(solution)/shard_map/reduce_scatter | solution.py:245
  913.6 88.6 %copy-start.11 = (bf16[1536,768]{1,0:T(8,128)(2,1)S(1)}, bf16[1536,768]{1,0:T(8,128)(2,1)}, u32[]{:S(2)}) copy-start(bf16[1536,768]{1,0:T(8,128)(2,1)} %param.29) | copy-start | bytes 7077892
  913.6 88.6 %copy-start.35 = (f32[1536]{0:T(1024)S(1)}, f32[1536]{0:T(1024)}, u32[]{:S(2)}) copy-start(f32[1536]{0:T(1024)} %copy-done.34) | copy-start | bytes 18436
  913.7 88.6 %copy-start.40 = (f32[768]{0:T(1024)S(1)}, f32[768]{0:T(1024)}, u32[]{:S(2)}) copy-start(f32[768]{0:T(1024)} %copy-done.39) | copy-start | bytes 9220
  913.7 130.1 %reduce-scatter.18.cloned.1.call-start = ((), (), s32[]{:S(2)}) async-start(), calls=%async_computation.13 | async-start | bytes 884736
  918.3 189.9 %reduce-scatter.20.cloned.1.call-start = ((), (), s32[]{:S(2)}) async-start(), calls=%async_computation.14 | async-start | bytes 442368
  1007.0 171.8 %reduce-scatter.16.cloned.1.call-start = ((), (), s32[]{:S(2)}) async-start(), calls=%async_computation.12 | async-start | bytes 2211840
  1020.5 235.4 %reduce-scatter.12.cloned.1.call-start = ((), (), s32[]{:S(2)}) async-start(), calls=%async_computation.10 | async-start | bytes 3538944 | tf_op jit(solution)/shard_map/reduce_scatter | solution.py:244
  1029.0 229.9 %copy-start.43 = (f32[1536]{0:T(1024)S(1)}, f32[1536]{0:T(1024)}, u32[]{:S(2)}) copy-start(f32[1536]{0:T(1024)} %get-tuple-element.798) | copy-start | bytes 18436
  1109.1 149.8 %copy-start.48 = (f32[2,96]{1,0:T(2,128)}, f32[2,96]{1,0:T(2,128)S(1)}, u32[]{:S(2)}) copy-start(f32[2,96]{1,0:T(2,128)S(1)} %copy.205) | copy-start | bytes 2308
  1258.9 47.5 %copy-start.22 = (f32[3,96,192]{1,2,0:T(8,128)S(1)}, f32[3,96,192]{1,2,0:T(8,128)}, u32[]{:S(2)}) copy-start(f32[3,96,192]{1,2,0:T(8,128)} %copy.193) | copy-start | bytes 663556
  1264.4 48.4 %copy-start.29 = (f32[192,96]{1,0:T(8,128)S(1)}, f32[192,96]{1,0:T(8,128)}, u32[]{:S(2)}) copy-start(f32[192,96]{1,0:T(8,128)} %param.33) | copy-start | bytes 221188
  1264.4 48.4 %copy-start.32 = (f32[192,96]{1,0:T(8,128)S(1)}, f32[192,96]{1,0:T(8,128)}, u32[]{:S(2)}) copy-start(f32[192,96]{1,0:T(8,128)} %param.39) | copy-start | bytes 221188
  1264.4 48.4 %copy-start.33 = (f32[192,96]{1,0:T(8,128)S(1)}, f32[192,96]{1,0:T(8,128)}, u32[]{:S(2)}) copy-start(f32[192,96]{1,0:T(8,128)} %param.45) | copy-start | bytes 221188
  1264.4 49.2 %copy-start.27 = (f32[512,96]{0,1:T(8,128)S(1)}, f32[512,96]{0,1:T(8,128)}, u32[]{:S(2)}) copy-start(f32[512,96]{0,1:T(8,128)} %param.35) | copy-start | bytes 589828
  1264.4 49.2 %copy-start.28 = (f32[512,96]{0,1:T(8,128)S(1)}, f32[512,96]{0,1:T(8,128)}, u32[]{:S(2)}) copy-start(f32[512,96]{0,1:T(8,128)} %reduce-scatter.14.cloned.1.call-done) | copy-start | bytes 589828
  1264.4 49.2 %copy-start.31 = (f32[512,96]{0,1:T(8,128)S(1)}, f32[512,96]{0,1:T(8,128)}, u32[]{:S(2)}) copy-start(f32[512,96]{0,1:T(8,128)} %param.41) | copy-start | bytes 589828
  1264.5 51.0 %copy-start.20 = (f32[2,96,512]{2,1,0:T(8,128)S(1)}, f32[2,96,512]{2,1,0:T(8,128)}, u32[]{:S(2)}) copy-start(f32[2,96,512]{2,1,0:T(8,128)} %param.34) | copy-start | bytes 1179652
  1264.5 51.0 %copy-start.21 = (f32[2,96,512]{2,1,0:T(8,128)S(1)}, f32[2,96,512]{2,1,0:T(8,128)}, u32[]{:S(2)}) copy-start(f32[2,96,512]{2,1,0:T(8,128)} %reduce-scatter.12.cloned.1.call-done) | copy-start | bytes 1179652
  (69 other events, 489.8 us)
Sparse Core Ops, SparseCore 0:
  273.6 92.6 all-reduce.7
  392.9 94.1 all-reduce.11
  490.0 55.8 all-reduce.9
  908.1 94.1 all-reduce.13
Sparse Core Ops, SparseCore 1:
  276.8 43.9 all-gather.2
  913.7 65.1 reduce-scatter.13
  982.4 61.3 reduce-scatter.17
  1047.6 60.6 reduce-scatter.19
  1112.3 66.5 reduce-scatter.15
  1182.9 72.9 reduce-scatter.11
where the time goes:
time: 1340 us; the launch traced here: 1330 us
  waiting for transfers between devices  498 us (37%)
  local copies, waits for them, and re-layouts  451 us (34%)
  blocking collectives  165 us (12%)
  matrix products  99.9 us (7%)
  other arithmetic  88 us (7%)
  between operations  21.8 us (2%)
    unnamed x13, waiting for transfers between devices  140 us
    another operation x24, local copies, waits for them, and re-layouts, toeplitz_rows(): tiled_flat = jnp.tile(padded, length)[:length * (2 * length - 1)]  100 us
    reshape x12, local copies, waits for them, and re-layouts, toeplitz_rows(): return tiled_flat.reshape(length, 2 * length - 1)[:, length - 1:]  92.6 us
    psum x1, waiting for transfers between devices, body(): d_normed_two = lax.psum(second_terms, 'narrow')  89.9 us
    psum x1, waiting for transfers between devices, body(): d_normed_one = lax.psum(first_terms, 'narrow')  83.8 us
    reduce_scatter x1, waiting for transfers between devices, body(): lax.psum_scatter(expand_grad, 'wide', scatter_dimension=1, tiled=True)  73.7 us
    psum x1, waiting for transfers between devices, body(): middle = input_float + lax.psum(attention_terms, 'narrow')  57.1 us
    psum x1, waiting for transfers between devices, body(): lax.psum(feedforward_terms.astype(jnp.bfloat16), 'narrow')  53.7 us
  transfers between devices with their start and end apart: 10, of which 8 were waited for; matrix products, arithmetic and copies ran while one was open for 5% of the time, Pallas kernels for 0%

commit v1 on v0

--- a/solution.py
+++ b/solution.py
@@ -14,6 +14,12 @@
 step_rates = (0.06, 0.3, 0.07, 0.06, 1.0, 0.3)
 decay_rates = (0.01, 0.01, 0.01, 0.01, 0.0, 0.0)
 masked_score = -1000000000.0
+
+
+def add_all(block, axis):
+    shards = lax.all_gather(block, axis, axis=0, tiled=False)
+    acc = shards.sum(axis=0)
+    return acc
 
 
 def bucket_of(offsets):
@@ -145,7 +151,7 @@
     attended, log_totals = lax.map(buffer_forward, (buffer_rows, segment_ids))
     attended = attended.reshape(tokens, head_width)
     attention_terms = jnp.dot(attended, output_all, preferred_element_type=jnp.float32)
-    middle = input_float + lax.psum(attention_terms, "narrow")
+    middle = input_float + add_all(attention_terms, "narrow")
     scale_two = rms_scale(middle)
     normed_two = (middle * scale_two * gain_two).astype(jnp.bfloat16)
     expand_flat = jnp.transpose(expand_all, (1, 0, 2)).reshape(model_width, 2 * hidden_local)

time: 1340 us -> 1460 us (1.090)
  waiting for transfers between devices: 498 us -> 614 us
    all_gather x0 -> x1, waiting for transfers between devices: none -> 81.9 us  [add_all(): shards = lax.all_gather(block, axis, axis=0, tiled=False)]
    psum x1 -> x0, waiting for transfers between devices: 57.1 us -> none  [body(): middle = input_float + lax.psum(attention_terms, 'narrow')]
    unnamed x13, waiting for transfers between devices: 140 us -> 194 us
    reduce_scatter x1, waiting for transfers between devices: 0.03 us -> 37.1 us  [body(): lax.psum_scatter(shrink_grad, 'wide', scatter_dimension=1, tiled=True)]
  transfers between devices with their start and end apart: 10 -> 10, of which waited for: 8 -> 9; matrix products, arithmetic and copies ran while one was open for 5% -> 16% of each run, Pallas kernels for 0% -> 0%
where the time goes in v1:
time: 1460 us; the launch traced here: 1450 us
  waiting for transfers between devices  614 us (42%)
  local copies, waits for them, and re-layouts  451 us (31%)
  blocking collectives  168 us (12%)
  other arithmetic  96.4 us (7%)
  matrix products  96.3 us (7%)
  between operations  20.7 us (1%)
    unnamed x13, waiting for transfers between devices  194 us
    another operation x24, local copies, waits for them, and re-layouts, toeplitz_rows(): tiled_flat = jnp.tile(padded, length)[:length * (2 * length - 1)]  100 us
    reshape x12, local copies, waits for them, and re-layouts, toeplitz_rows(): return tiled_flat.reshape(length, 2 * length - 1)[:, length - 1:]  92.6 us
    psum x1, waiting for transfers between devices, body(): d_normed_two = lax.psum(second_terms, 'narrow')  89.8 us
    psum x1, waiting for transfers between devices, body(): d_normed_one = lax.psum(first_terms, 'narrow')  83.8 us
    all_gather x1, waiting for transfers between devices, add_all(): shards = lax.all_gather(block, axis, axis=0, tiled=False)  81.9 us
    reduce_scatter x1, waiting for transfers between devices, body(): lax.psum_scatter(expand_grad, 'wide', scatter_dimension=1, tiled=True)  73.8 us
    psum x1, waiting for transfers between devices, body(): lax.psum(feedforward_terms.astype(jnp.bfloat16), 'narrow')  53.6 us
  transfers between devices with their start and end apart: 10, of which 9 were waited for; matrix products, arithmetic and copies ran while one was open for 16% of the time, Pallas kernels for 0%

profile of v1, /device:TPU:0, one launch (start us, length us, event | category | flops | bytes accessed | tf_op | source)
XLA Modules:
  0.0 1449.0 jit_solution(10481369356298266114)
XLA Ops:
  10.9 22.1 %all-gather.1 = bf16[8,96,2]{1,2,0:T(2,128)(2,1)S(1)} all-gather(bf16[1,96,2]{1,2,0:T(2,128)(2,1)S(1)} %convert_bitcast_fusion), channel_id=1, replica_groups=mesh['wide'=8,'narrow'=4] {'wide'}, dimensions={0}, use_global_device_ids=true | all-gather | bytes 3456 | tf_op jit(solution)/shard_map/all_gather | solution.py:99
  37.7 43.0 %all_gather.22 = bf16[3,768,192]{2,0,1:T(4,128)(2,1)} all-gather(bf16[3,96,192]{2,0,1:T(4,128)(2,1)S(1)} %copy.181), channel_id=1, replica_groups=mesh['wide'=8,'narrow'=4] {'wide'}, dimensions={1}, use_global_device_ids=true | all-gather | bytes 995328 | tf_op jit(solution)/shard_map/all_gather | solution.py:95
  88.3 152.8 %while.65 = (s32[]{:T(128)}, bf16[2,768,192]{1,2,0:T(8,128)(2,1)}, f32[2,3,768]{2,1,0:T(4,128)}, bf16[2,768,576]{1,2,0:T(8,128)(2,1)}, s32[2,768]{1,0:T(2,128)},...) while((s32[]{:T(128)}, bf16[2,768,192]{1,2,0:T(8,128)(2,1)}, ...), condition=%wide.region_8.9_spmd, body=%wide.region_3.8_spmd.sunk | while | flops 155763456 | bytes 47086936 | solution.py:151
  90.3 73.0 %while.68 = (s32[]{:T(128)}, bf16[3,768,64]{1,2,0:T(8,128)(2,1)S(1)}, f32[3,768]{1,0:T(4,128)S(1)}, bf16[3,768,64]{1,2,0:T(8,128)(2,1)S(1)}, bf16[3,768,64]{1,2,...) while((s32[]{:T(128)}, ...), condition=%wide.region_7.7_spmd.clone, body=%wide.region_4.6_spmd.clone.sunk | while | flops 155763456 | bytes 42930292 | solution.py:148
  99.5 7.7 reshape.317
  123.9 7.7 reshape.317
  148.2 7.7 reshape.317
  166.7 73.0 %while.68 = (s32[]{:T(128)}, bf16[3,768,64]{1,2,0:T(8,128)(2,1)S(1)}, f32[3,768]{1,0:T(4,128)S(1)}, bf16[3,768,64]{1,2,0:T(8,128)(2,1)S(1)}, bf16[3,768,64]{1,2,...) while((s32[]{:T(128)}, ...), condition=%wide.region_7.7_spmd.clone, body=%wide.region_4.6_spmd.clone.sunk | while | flops 155763456 | bytes 42930292 | solution.py:148
  175.9 7.7 reshape.317
  200.3 7.7 reshape.317
  243.2 31.1 %all_gather.23 = bf16[192,768]{0,1:T(8,128)(2,1)S(1)} all-gather(bf16[192,96]{0,1:T(8,128)(2,1)S(1)} %copy.186), channel_id=1, replica_groups=mesh['wide'=8,'narrow'=4] {'wide'}, dimensions={1}, use_global_device_ids=true | all-gather | bytes 331776 | tf_op jit(solution)/shard_map/all_gather | solution.py:96
  278.2 32.0 %all_gather.27 = bf16[512,768]{0,1:T(8,128)(2,1)S(1)} all-gather(bf16[512,96]{0,1:T(8,128)(2,1)S(1)} %convert_element_type.180), channel_id=1, replica_groups=mesh['wide'=8,'narrow'=4] {'wide'}, dimensions={1}, use_global_device_ids=true | all-gather | bytes 884736 | tf_op jit(solution)/shard_map/all_gather | solution.py:98
  315.2 81.9 %all-gather.7.cloned.1.call-done = f32[6144,768]{1,0:T(8,128)} async-done(((f32[1536,768]{1,0:T(8,128)}), f32[6144,768]{1,0:T(8,128)}) %all-gather.7.cloned.1.call-update) | async-done | bytes 18874384 | tf_op jit(solution)/shard_map/all_gather | solution.py:20
  397.0 10.5 reduce_sum.170
  429.4 89.8 %all-reduce.9.cloned.1.call-done = f32[1536,768]{1,0:T(8,128)} async-done(((f32[1536,768]{1,0:T(8,128)}), f32[1536,768]{1,0:T(8,128)}) %all-reduce.9.cloned.1.call-update) | async-done | bytes 4718608 | tf_op jit(solution)/shard_map/psum | solution.py:180
  524.3 53.6 %all-reduce.7.cloned.1.call-done = bf16[1536,768]{1,0:T(8,128)(2,1)} async-done(((bf16[1536,768]{1,0:T(8,128)(2,1)}), bf16[1536,768]{1,0:T(8,128)(2,1)}) %all-reduce.7.cloned.1.call-update) | async-done | bytes 2359312 | tf_op jit(solution)/shard_map/psum | solution.py:167
  586.5 346.4 %while.67 = (s32[]{:T(128)}, bf16[2,768,576]{1,2,0:T(8,128)(2,1)}, f32[2,3,1535]{2,1,0:T(4,128)}, bf16[2,768,576]{1,2,0:T(8,128)(2,1)}, f32[2,3,768]{2,1,0:T(4,1...) while((s32[]{:T(128)}, bf16[2,768,576]{1,2,0:T(8,128)(2,1)}, ...), condition=%wide.region_19.20_spmd, body=%wide.region_14.19_spmd.sunk | while | flops 386777856 | bytes 102011568 | solution.py:226
  591.0 165.1 %while.69 = (s32[]{:T(128)}, bf16[3,3,768,64]{2,3,0,1:T(8,128)(2,1)}, f32[3,1535]{1,0:T(4,128)}, bf16[3,768,64]{1,2,0:T(8,128)(2,1)S(1)}, bf16[3,768,64]{1,2,0:T...) while((s32[]{:T(128)}, ...), condition=%wide.region_18.18_spmd.clone, body=%wide.region_15.17_spmd.clone.sunk | while | flops 386777856 | bytes 96039304 | solution.py:221
  633.6 8.2 reshape.316
  688.6 8.2 reshape.316
  743.6 8.2 reshape.316
  763.9 165.1 %while.69 = (s32[]{:T(128)}, bf16[3,3,768,64]{2,3,0,1:T(8,128)(2,1)}, f32[3,1535]{1,0:T(4,128)}, bf16[3,768,64]{1,2,0:T(8,128)(2,1)S(1)}, bf16[3,768,64]{1,2,0:T...) while((s32[]{:T(128)}, ...), condition=%wide.region_18.18_spmd.clone, body=%wide.region_15.17_spmd.clone.sunk | while | flops 386777856 | bytes 96039304 | solution.py:221
  806.5 8.2 reshape.316
  861.5 8.2 reshape.316
  916.5 8.2 reshape.316
  950.5 83.8 %all-reduce.11.cloned.1.call-done = f32[1536,768]{1,0:T(8,128)} async-done(((f32[1536,768]{1,0:T(8,128)}), f32[1536,768]{1,0:T(8,128)}) %all-reduce.11.cloned.1.call-update) | async-done | bytes 4718608 | tf_op jit(solution)/shard_map/psum | solution.py:236
  1065.6 37.1 %reduce-scatter.14.cloned.1.call-done = f32[512,96]{0,1:T(8,128)} async-done(((f32[512,768]{0,1:T(8,128)}), f32[512,96]{0,1:T(8,128)}) %reduce-scatter.14.cloned.1.call-update) | async-done | bytes 196624 | tf_op jit(solution)/shard_map/reduce_scatter | solution.py:251
  1104.2 63.5 %reduce-scatter.18.cloned.1.call-done = f32[96,192]{1,0:T(8,128)} async-done(((f32[768,192]{1,0:T(8,128)}), f32[96,192]{1,0:T(8,128)}) %reduce-scatter.18.cloned.1.call-update) | async-done | bytes 73744
  1169.3 62.7 %reduce-scatter.20.cloned.1.call-done = f32[96,2]{1,0:T(8,128)} async-done(((f32[768,2]{1,0:T(8,128)}), f32[96,2]{1,0:T(8,128)}) %reduce-scatter.20.cloned.1.call-update) | async-done | bytes 784
  1234.2 67.7 %reduce-scatter.16.cloned.1.call-done = f32[96,576]{1,0:T(8,128)} async-done(((f32[768,576]{1,0:T(8,128)}), f32[96,576]{1,0:T(8,128)}) %reduce-scatter.16.cloned.1.call-update) | async-done | bytes 221200
  1305.1 73.8 %reduce-scatter.12.cloned.1.call-done = f32[2,96,512]{2,1,0:T(8,128)} async-done(((f32[2,768,512]{2,1,0:T(8,128)}), f32[2,96,512]{2,1,0:T(8,128)}) %reduce-scatter.12.cloned.1.call-update) | async-done | bytes 393232 | tf_op jit(solution)/shard_map/reduce_scatter | solution.py:250
  1387.5 39.9 %all-reduce.2 = (f32[]{:T(128)}, f32[32,12]{0,1:T(8,128)S(1)}) all-reduce(f32[]{:T(128)S(6)} %add.319, f32[32,12]{0,1:T(8,128)S(1)} %dynamic_update_slice.47), channel_id=1, replica_groups=mesh['wide'=8,'narrow'=4] {'wide','narrow'}, use_global_device_ids=true, to_apply=%region_34.35 | all-reduce | flops 385 | bytes 3080 | tf_op jit(solution)/shard_map/psum | solution.py:265
  (521 shorter events, 546.4 us)
Async XLA Ops:
  7.2 30.4 %copy-start.22 = (f32[3,96,192]{2,1,0:T(8,128)S(1)}, f32[3,96,192]{2,1,0:T(8,128)}, u32[]{:S(2)}) copy-start(f32[3,96,192]{2,1,0:T(8,128)} %param.32) | copy-start | bytes 663556
  7.2 303.1 %all-gather.5.cloned.1.call-start = ((), (), s32[]{:S(2)}) async-start(), calls=%async_computation.5 | async-start | bytes 1769472 | tf_op jit(solution)/shard_map/all_gather | solution.py:97
  9.3 387.7 %all-gather.7.cloned.1.call-start = ((), (), s32[]{:S(2)}) async-start(), calls=%async_computation.11 | async-start | bytes 23592960 | tf_op jit(solution)/shard_map/all_gather | solution.py:20
  9.4 77.0 %copy-start.47 = (s32[1535]{0:T(1024)}, s32[1535]{0:T(1024)S(1)}, u32[]{:S(2)}) copy-start(s32[1535]{0:T(1024)S(1)} %fusion.86) | copy-start | bytes 18424
  33.8 49.5 %copy-start.39 = (f32[768]{0:T(1024)}, f32[768]{0:T(1024)S(1)}, u32[]{:S(2)}) copy-start(f32[768]{0:T(1024)S(1)} %get-tuple-element.696) | copy-start | bytes 9220
  34.6 48.7 %copy-start.10 = (bf16[1536,768]{1,0:T(8,128)(2,1)S(1)}, bf16[1536,768]{1,0:T(8,128)(2,1)}, u32[]{:S(2)}) copy-start(bf16[1536,768]{1,0:T(8,128)(2,1)} %param.29) | copy-start | bytes 7077892
  37.6 47.4 %copy-start.34 = (f32[1536]{0:T(1024)}, f32[1536]{0:T(1024)S(1)}, u32[]{:S(2)}) copy-start(f32[1536]{0:T(1024)S(1)} %get-tuple-element.799) | copy-start | bytes 18436
  243.2 31.1 %copy-start.13 = (bf16[2,24,8,768]{3,2,0,1:T(8,128)(2,1)}, bf16[2,24,8,768]{3,2,0,1:T(8,128)(2,1)S(1)}, u32[]{:S(2)}) copy-start(bf16[2,24,8,768]{3,2,0,1:T(8,128)(2,1)S(1)} %copy.221) | copy-start | bytes 1769476
  277.3 241.9 %all-reduce.9.cloned.1.call-start = ((), (), s32[]{:S(2)}) async-start(), calls=%async_computation.7 | async-start | bytes 9437184 | tf_op jit(solution)/shard_map/psum | solution.py:180
  411.4 166.5 %copy-start.36 = (f32[1536]{0:T(1024)}, f32[1536]{0:T(1024)S(1)}, u32[]{:S(2)}) copy-start(f32[1536]{0:T(1024)S(1)} %get-tuple-element.801) | copy-start | bytes 18436
  425.0 152.8 %all-reduce.7.cloned.1.call-start = ((), (), s32[]{:S(2)}) async-start(), calls=%async_computation.6 | async-start | bytes 4718592 | tf_op jit(solution)/shard_map/psum | solution.py:167
  429.3 605.0 %all-reduce.11.cloned.1.call-start = ((), (), s32[]{:S(2)}) async-start(), calls=%async_computation.8 | async-start | bytes 9437184 | tf_op jit(solution)/shard_map/psum | solution.py:236
  429.4 148.4 %copy-start.44 = (f32[1536]{0:T(1024)S(1)}, f32[1536]{0:T(1024)}, u32[]{:S(2)}) copy-start(f32[1536]{0:T(1024)} %get-tuple-element.800) | copy-start | bytes 18436
  940.1 162.6 %reduce-scatter.14.cloned.1.call-start = ((), (), s32[]{:S(2)}) async-start(), calls=%async_computation.10 | async-start | bytes 1769472 | tf_op jit(solution)/shard_map/reduce_scatter | solution.py:251
  945.7 88.6 %copy-start.12 = (bf16[1536,768]{1,0:T(8,128)(2,1)S(1)}, bf16[1536,768]{1,0:T(8,128)(2,1)}, u32[]{:S(2)}) copy-start(bf16[1536,768]{1,0:T(8,128)(2,1)} %param.29) | copy-start | bytes 7077892
  945.7 88.6 %copy-start.35 = (f32[1536]{0:T(1024)S(1)}, f32[1536]{0:T(1024)}, u32[]{:S(2)}) copy-start(f32[1536]{0:T(1024)} %copy-done.34) | copy-start | bytes 18436
  945.7 88.6 %copy-start.40 = (f32[768]{0:T(1024)S(1)}, f32[768]{0:T(1024)}, u32[]{:S(2)}) copy-start(f32[768]{0:T(1024)} %copy-done.39) | copy-start | bytes 9220
  945.7 222.0 %reduce-scatter.18.cloned.1.call-start = ((), (), s32[]{:S(2)}) async-start(), calls=%async_computation.13 | async-start | bytes 884736
  950.4 281.6 %reduce-scatter.20.cloned.1.call-start = ((), (), s32[]{:S(2)}) async-start(), calls=%async_computation.14 | async-start | bytes 442368
  1039.1 262.7 %reduce-scatter.16.cloned.1.call-start = ((), (), s32[]{:S(2)}) async-start(), calls=%async_computation.12 | async-start | bytes 2211840
  1052.5 326.4 %reduce-scatter.12.cloned.1.call-start = ((), (), s32[]{:S(2)}) async-start(), calls=%async_computation.9 | async-start | bytes 3538944 | tf_op jit(solution)/shard_map/reduce_scatter | solution.py:250
  1061.1 320.8 %copy-start.43 = (f32[1536]{0:T(1024)S(1)}, f32[1536]{0:T(1024)}, u32[]{:S(2)}) copy-start(f32[1536]{0:T(1024)} %get-tuple-element.798) | copy-start | bytes 18436
  1232.9 149.0 %copy-start.49 = (f32[2,96]{1,0:T(2,128)}, f32[2,96]{1,0:T(2,128)S(1)}, u32[]{:S(2)}) copy-start(f32[2,96]{1,0:T(2,128)S(1)} %copy.205) | copy-start | bytes 2308
  1381.9 47.4 %copy-start.21 = (f32[3,96,192]{1,2,0:T(8,128)S(1)}, f32[3,96,192]{1,2,0:T(8,128)}, u32[]{:S(2)}) copy-start(f32[3,96,192]{1,2,0:T(8,128)} %copy.193) | copy-start | bytes 663556
  1387.5 48.4 %copy-start.29 = (f32[192,96]{1,0:T(8,128)S(1)}, f32[192,96]{1,0:T(8,128)}, u32[]{:S(2)}) copy-start(f32[192,96]{1,0:T(8,128)} %param.33) | copy-start | bytes 221188
  1387.5 48.4 %copy-start.32 = (f32[192,96]{1,0:T(8,128)S(1)}, f32[192,96]{1,0:T(8,128)}, u32[]{:S(2)}) copy-start(f32[192,96]{1,0:T(8,128)} %param.39) | copy-start | bytes 221188
  1387.5 48.4 %copy-start.33 = (f32[192,96]{1,0:T(8,128)S(1)}, f32[192,96]{1,0:T(8,128)}, u32[]{:S(2)}) copy-start(f32[192,96]{1,0:T(8,128)} %param.45) | copy-start | bytes 221188
  1387.5 49.2 %copy-start.27 = (f32[512,96]{0,1:T(8,128)S(1)}, f32[512,96]{0,1:T(8,128)}, u32[]{:S(2)}) copy-start(f32[512,96]{0,1:T(8,128)} %param.35) | copy-start | bytes 589828
  1387.5 49.2 %copy-start.28 = (f32[512,96]{0,1:T(8,128)S(1)}, f32[512,96]{0,1:T(8,128)}, u32[]{:S(2)}) copy-start(f32[512,96]{0,1:T(8,128)} %reduce-scatter.14.cloned.1.call-done) | copy-start | bytes 589828
  1387.5 49.2 %copy-start.31 = (f32[512,96]{0,1:T(8,128)S(1)}, f32[512,96]{0,1:T(8,128)}, u32[]{:S(2)}) copy-start(f32[512,96]{0,1:T(8,128)} %param.41) | copy-start | bytes 589828
  1387.5 51.0 %copy-start.19 = (f32[2,96,512]{2,1,0:T(8,128)S(1)}, f32[2,96,512]{2,1,0:T(8,128)}, u32[]{:S(2)}) copy-start(f32[2,96,512]{2,1,0:T(8,128)} %param.34) | copy-start | bytes 1179652
  1387.5 51.0 %copy-start.20 = (f32[2,96,512]{2,1,0:T(8,128)S(1)}, f32[2,96,512]{2,1,0:T(8,128)}, u32[]{:S(2)}) copy-start(f32[2,96,512]{2,1,0:T(8,128)} %reduce-scatter.12.cloned.1.call-done) | copy-start | bytes 1179652
  (70 other events, 538.4 us)
Sparse Core Ops, SparseCore 0:
  10.8 64.3 all-gather.4
  277.4 119.5 all-gather.6
  425.1 94.0 all-reduce.8
  522.0 55.8 all-reduce.6
  940.2 94.0 all-reduce.10
  1037.6 65.0 reduce-scatter.13
  1106.3 61.3 reduce-scatter.17
  1171.6 60.4 reduce-scatter.19
  1236.1 65.6 reduce-scatter.15
  1305.7 73.1 reduce-scatter.11
